TPU v7x, 1024 devices: a whole 8x8x8 slice. The times are simulated.
1024 devices in a mesh: expert: 64 (over y, x), dp: 16 (over z, core).
Axes of the slice: x: 8, y: 8, z: 8, core: 2. Of those that a mesh axis runs over, the one named last changes fastest.
Arguments:
- tokens: bfloat16 [16384, 2048], P(('dp', 'expert')), may hold values from -6 to 6
- cotangent: bfloat16 [16384, 8, 384], P(('dp', 'expert')), may hold values from -1 to 1
- expert_ids: int32 [16384, 8], P(('dp', 'expert')), may hold values from 0 to 31, all different within a row; in each aligned block of 16 rows (0 to 15, 16 to 31, ...) at most 5 rows name the same one
- placement: int32 [64], replicated, may hold values from 0 to 31, as said below
- master: float32 [32, 1572864], P(None, ('dp', 'expert')), may hold values from -0.125 to 0.125
- first_moment: float32 [32, 1572864], P(None, ('dp', 'expert')), may hold values from -12 to 12
- second_moment: float32 [32, 1572864], P(None, ('dp', 'expert')), may hold values from 1 to 30
Outputs:
- new_master: float32 [32, 1572864], P(None, ('dp', 'expert'))
- new_first: float32 [32, 1572864], P(None, ('dp', 'expert'))
- new_second: float32 [32, 1572864], P(None, ('dp', 'expert'))
- replica_grad: float32 [64, 384, 4096], P('expert', 'dp')
Inputs may be any that keep to these rules, and one draw needn't show every extreme that they name: `expert_ids`: among the tokens of one device no expert is named more than 5 times; some device names some expert exactly 5 times. `placement`: every one of the 32 experts holds at least one of the 64 slots.
All inputs are finite; a program needn't handle non-finite values.
Results may differ from a plain program's by a relative error of at most 0.017.
Values may be sent and summed in bfloat16 or wider, within the bound.
No kernel may reach another device: no remote copies, remote signals or barrier semaphores. Data moves between devices by JAX's collectives and lax.ppermute only.
A program may use at most 64 MiB of HBM per device.

v0:
```python
import functools

import jax
import jax.numpy as jnp
from jax import lax
from jax.experimental import pallas as pl
from jax.experimental.pallas import tpu as pltpu
from jax.sharding import Mesh, PartitionSpec as P


MOST = 5
LANES = 128
CORES = 2
FAR = 3
GRANT = 24 << 20


beta_first = 0.9
beta_second = 0.95
learning_rate = 0.01
decay_rate = 0.1
epsilon = 1e-08
adam_steps = 20.0


def adamw_update(master, first_moment, second_moment, grads):
    new_first = beta_first * first_moment + (1.0 - beta_first) * grads
    new_second = beta_second * second_moment + (1.0 - beta_second) * grads * grads
    corr_first = 1.0 - beta_first**adam_steps
    corr_second = 1.0 - beta_second**adam_steps
    update = (
        new_first / corr_first / (jnp.sqrt(new_second / corr_second) + epsilon)
        + decay_rate * master
    )
    return (master - learning_rate * update, new_first, new_second)


def offset_of(block, planes):
    return jnp.where(block % 2 == 1, (planes - 1 - block) // 2, -((planes - block) // 2))


def store_grads(outs, parts, rows_refs, piece_rows, width):
    tile = 512
    units = len(outs) * piece_rows
    for start in range(0, width, tile):
        cols = slice(start, start + tile)
        total = jnp.dot(parts[0], rows_refs[0][:, cols], preferred_element_type=jnp.float32)
        total += jnp.dot(parts[1], rows_refs[1][:, cols], preferred_element_type=jnp.float32)
        total = total.reshape(2, units, tile)
        for at, out in enumerate(outs):
            rows = slice(at * piece_rows, (at + 1) * piece_rows)
            out[:, start : start + tile] = total[0, rows].astype(jnp.bfloat16)
            out[:, width + start : width + start + tile] = total[1, rows].astype(jnp.bfloat16)


def grads_kernel(planes, piece_rows, first_block, count, place, x_own, x_other, *refs):
    f32, bf16 = jnp.float32, jnp.bfloat16
    pieces, outs, weights = refs[:count], refs[count : 2 * count], refs[2 * count]
    units, width = weights.shape[0] // 2, weights.shape[1]
    for at, piece in enumerate(pieces):
        lines = slice(at * piece_rows, (at + 1) * piece_rows)
        weights[lines, :] = piece[:, :width]
        lines = slice(units + at * piece_rows, units + (at + 1) * piece_rows)
        weights[lines, :] = piece[:, width:]
    hidden = planes * piece_rows * CORES
    rows = x_own.shape[0]
    sources = rows // (MOST + 1)
    across = (((1,), (1,)), ((), ()))

    def iota(shape, dim):
        return lax.broadcasted_iota(jnp.int32, shape, dim)

    def hot(mask):
        return mask.astype(f32).astype(bf16)

    unit = iota((units, hidden), 0)
    block = unit // piece_rows
    plane = place[0] + offset_of(block + first_block, planes) + planes
    plane = jnp.where(plane >= planes, plane - planes, plane)
    plane = jnp.where(plane >= planes, plane - planes, plane)
    column = (plane * CORES + place[1]) * piece_rows + unit - block * piece_rows
    choose = hot(iota((units, hidden), 1) == column)
    last = hot(iota((sources, rows), 1) == iota((sources, rows), 0) * (MOST + 1) + MOST)
    parts = []
    for x_ref in (x_own, x_other):
        packed = jnp.dot(last, x_ref[:, : MOST * hidden], preferred_element_type=f32).astype(bf16)
        dh = jnp.zeros((units, rows), f32)
        for at in range(MOST):
            mine = packed[:, at * hidden : (at + 1) * hidden]
            mine = lax.dot_general(choose, mine, across, preferred_element_type=f32).astype(bf16)
            spread = hot(iota((sources, rows), 1) == iota((sources, rows), 0) * (MOST + 1) + at)
            dh += jnp.dot(mine, spread, preferred_element_type=f32)
        both = lax.dot_general(weights[...], x_ref[...], across, preferred_element_type=f32)
        gate, up = both[:units], both[units:]
        sig = jax.nn.sigmoid(gate)
        d_gate = dh * up * (sig * (1.0 + gate * (1.0 - sig)))
        d_up = dh * (gate * sig)
        parts.append(jnp.concatenate([d_gate, d_up], axis=0).astype(bf16))
    store_grads(outs, parts, (x_own, x_other), piece_rows, width)


def swiglu_grads(planes, piece_rows, first_block, place, x_own, x_other, pieces):
    bf16 = jnp.bfloat16
    vmem, smem = pl.BlockSpec(memory_space=pltpu.VMEM), pl.BlockSpec(memory_space=pltpu.SMEM)
    rows, width = x_own.shape
    count = len(pieces)
    units = count * piece_rows
    block = jax.ShapeDtypeStruct((piece_rows, 2 * width), bf16)
    return pl.pallas_call(
        functools.partial(grads_kernel, planes, piece_rows, first_block, count),
        out_shape=[block] * count,
        in_specs=[smem] + [vmem] * (2 + count),
        out_specs=[vmem] * count,
        scratch_shapes=[pltpu.VMEM((2 * units, width), bf16)],
        compiler_params=pltpu.CompilerParams(vmem_limit_bytes=GRANT),
        cost_estimate=pl.CostEstimate(
            flops=8 * CORES * rows * units * width, bytes_accessed=5 << 20, transcendentals=0
        ),
    )(place, x_own, x_other, *pieces)


def shift(value, planes, by):
    return lax.ppermute(value, "z", [(i, (i - by) % planes) for i in range(planes)])


def shift_by_core(value, planes, by):
    pairs = []
    for i in range(planes):
        pairs.append((i * CORES, (i - by) % planes * CORES))
        pairs.append((i * CORES + 1, (i + by) % planes * CORES + 1))
    return lax.ppermute(value, ("z", "c"), pairs)


def gather_planes(piece, planes):
    pieces = [shift(piece, planes, planes // 2)]
    by = planes // 2 - 1
    pieces += [shift(piece, planes, by), shift(piece, planes, -by)]
    for by in range(planes // 2 - 2, 0, -1):
        pieces += [shift(piece, planes, by), shift(piece, planes, -by)]
    return pieces + [piece]


def local(tokens, cotangent, expert_ids, placement, master, first_moment, second_moment):
    bf16, f32, i32 = jnp.bfloat16, jnp.float32, jnp.int32
    slots = lax.axis_size("expert")
    planes = lax.axis_size("z")
    source_index = lax.axis_index("expert")
    core = lax.axis_index("c")
    expert_count, shard_width = master.shape
    token_rows, width = tokens.shape
    top_count = expert_ids.shape[1]
    hidden = cotangent.shape[2]
    assigned = token_rows * top_count
    piece_rows = shard_width * slots // (2 * width)
    rows = slots * MOST
    expert_range = jnp.arange(expert_count, dtype=i32)
    slot_range = jnp.arange(slots, dtype=i32)

    slot_hot = placement[:, None] == expert_range[None, :]
    send_weight = jnp.dot(
        slot_hot.astype(bf16), master.astype(bf16), preferred_element_type=f32
    ).astype(bf16)
    send_weight = send_weight.reshape(slots, shard_width // LANES, LANES)
    recv_weight = lax.all_to_all(send_weight, "expert", split_axis=0, concat_axis=0, tiled=True)

    replicas = jnp.sum(slot_hot.astype(i32), axis=0)
    earlier_same = (slot_range[:, None] > slot_range[None, :]) & (
        placement[:, None] == placement[None, :]
    )
    slot_rank = jnp.sum(earlier_same.astype(i32), axis=1)
    wanted = jnp.mod(source_index, replicas)
    target_hot = slot_hot & (slot_rank[:, None] == wanted[None, :])
    target_slot = jnp.sum(jnp.where(target_hot, slot_range[:, None], 0), axis=0)
    flat_ids = expert_ids.reshape(assigned)
    expert_hot = flat_ids[:, None] == expert_range[None, :]
    copy_range = jnp.arange(assigned, dtype=i32)
    before = (copy_range[:, None] > copy_range[None, :]) & (flat_ids[:, None] == flat_ids[None, :])
    position = jnp.sum(before.astype(i32), axis=1)
    destination = jnp.sum(jnp.where(expert_hot, target_slot[None, :], 0), axis=1)
    send_row = destination * MOST + position
    row_match = jnp.arange(rows, dtype=i32)[:, None] == send_row[None, :]
    pick = row_match.astype(bf16)
    token_of = (copy_range[:, None] // top_count == jnp.arange(token_rows, dtype=i32)[None, :])
    token_pick = jnp.dot(pick, token_of.astype(bf16), preferred_element_type=f32).astype(bf16)
    send_x = jnp.dot(token_pick, tokens, preferred_element_type=f32).astype(bf16)
    send_dh = jnp.dot(
        pick, cotangent.reshape(assigned, hidden), preferred_element_type=f32
    ).astype(bf16)
    x_rows = MOST * width // LANES
    dh_rows = MOST * hidden // LANES
    spare = -(x_rows + dh_rows) % 16
    send = jnp.concatenate(
        [
            send_x.reshape(slots, x_rows, LANES),
            send_dh.reshape(slots, dh_rows, LANES),
            jnp.zeros((slots, spare, LANES), bf16),
        ],
        axis=1,
    )
    send, recv_weight = lax.optimization_barrier((send, recv_weight))
    recv = lax.all_to_all(send, "expert", split_axis=0, concat_axis=0, tiled=True)
    other = lax.ppermute(recv, "c", [(0, 1), (1, 0)])

    own_piece = recv_weight.reshape(piece_rows, 2 * width)
    pieces = gather_planes(own_piece, planes)

    group = MOST + 1
    place = jnp.stack([lax.axis_index("z"), core])
    x_own = recv.reshape(slots * group, width)
    x_other = other.reshape(slots * group, width)
    far = swiglu_grads(planes, piece_rows, 0, place, x_own, x_other, pieces[:FAR])
    relayed = shift_by_core(far[0], planes, -2)
    parts = [shift(far[1], planes, -3), shift(far[2], planes, 3)]
    near = swiglu_grads(planes, piece_rows, FAR, place, x_own, x_other, pieces[FAR:])
    up2, down2, up1, down1, own = near
    more = relayed.astype(f32)
    up2 = (up2.astype(f32) + jnp.where(core == 0, more, 0.0)).astype(bf16)
    down2 = (down2.astype(f32) + jnp.where(core == 0, 0.0, more)).astype(bf16)
    parts += [shift(up2, planes, -2), shift(down2, planes, 2)]
    parts += [shift(up1, planes, -1), shift(down1, planes, 1)]
    summed = own.astype(f32)
    for part in parts:
        summed = summed + part.astype(f32)
    replica_grad = summed[None]

    outgoing = summed.astype(bf16).reshape(slots, shard_width // LANES, LANES)
    incoming = lax.all_to_all(outgoing, "expert", split_axis=0, concat_axis=0, tiled=True)
    incoming, replica_grad = lax.optimization_barrier((incoming, replica_grad))
    grads = lax.dot_general(
        slot_hot.astype(bf16),
        incoming.reshape(slots, shard_width),
        (((0,), (0,)), ((), ())),
        preferred_element_type=f32,
    )
    new_master, new_first, new_second = adamw_update(master, first_moment, second_moment, grads)
    return (new_master, new_first, new_second, replica_grad)


def solution(mesh):
    slots, dp = mesh.shape["expert"], mesh.shape["dp"]
    split = Mesh(
        mesh.devices.reshape(slots, dp // CORES, CORES), ("expert", "z", "c")
    )
    shard = ("z", "c", "expert")
    return jax.shard_map(
        local,
        mesh=split,
        in_specs=(
            P(shard, None),
            P(shard, None, None),
            P(shard, None),
            P(),
            P(None, shard),
            P(None, shard),
            P(None, shard),
        ),
        out_specs=(
            P(None, shard),
            P(None, shard),
            P(None, shard),
            P("expert", ("z", "c"), None),
        ),
        check_vma=False,
    )
```

profile of v0, /device:TPU:2, one launch (start us, length us, event | category | flops | bytes accessed | tf_op | source)
XLA Modules:
  0.0 209.5 jit_solution(13554961446643996923)
XLA Ops:
  0.6 1.2 convolution_convert_fusion.1
  1.9 0.9 reshape.99
  2.7 17.2 %all-to-all-start = ((bf16[64,12,128]{2,1,0:T(8,128)(2,1)}), bf16[64,12,128]{2,1,0:T(8,128)(2,1)S(1)}, u32[]{:S(2)}, u32[]{:S(2)}) async-start(bf16[64,12,128]{2,1,0:T(8,128)(2,1)} %reshape.99), calls=%async_computation | async-start | bytes 524288 | tf_op jit(solution)/shard_map/all_to_all | solution.py:164
  20.0 0.9 convert_reduce_fusion.1
  20.9 0.8 convert_reduce_fusion.2
  21.6 0.8 copy.13
  22.5 0.2 convert_reduce_fusion
  22.8 0.8 select_reduce_fusion.1
  23.7 1.6 convolution_convert_fusion
  25.4 0.2 convolution_convert_fusion.2
  25.8 0.6 reshape.96
  26.5 0.4 maximum_maximum_fusion
  26.9 6.2 %all-to-all-done = bf16[64,12,128]{2,1,0:T(8,128)(2,1)S(1)} async-done(((bf16[64,12,128]{2,1,0:T(8,128)(2,1)}), bf16[64,12,128]{2,1,0:T(8,128)(2,1)S(1)}, u32[]{:S(2)}, u32[]{:S(2)}) %all-to-all-start) | async-done | bytes 196640 | tf_op jit(solution)/shard_map/all_to_all | solution.py:164
  33.1 42.7 %all_to_all.15 = bf16[64,96,128]{2,1,0:T(8,128)(2,1)S(1)} all-to-all(bf16[64,96,128]{2,1,0:T(8,128)(2,1)S(1)} %maximum_maximum_fusion), channel_id=1, replica_groups=mesh['expert'=64,'z'=8,'c'=2] {'expert'}, dimensions={0} | all-to-all | bytes 3145728 | tf_op jit(solution)/shard_map/all_to_all | solution.py:201
  75.8 1.9 collective-permute-start
  77.7 0.9 reshape.102.refs_4_
  78.6 14.8 %collective-permute-start.5 = (bf16[24,4096]{1,0:T(8,128)(2,1)}, bf16[24,4096]{1,0:T(8,128)(2,1)S(1)}, u32[]{:S(2)}, u32[]{:S(2)}) collective-permute-start(bf16[24,4096]{1,0:T(8,128)(2,1)} %reshape.102.refs_4_), channel_id=1, source_target_pairs={{0,8},{2,10},{4,12},{6,14},{8,0},{10,2},{12,4},{14,6},{1,9},{3,11}... | collective-permute-start | bytes 589832 | tf_op jit(solution)/shard_map/ppermute | solution.py:123
  93.4 2.8 %collective-permute-start.6 = (bf16[24,4096]{1,0:T(8,128)(2,1)}, bf16[24,4096]{1,0:T(8,128)(2,1)S(1)}, u32[]{:S(2)}, u32[]{:S(2)}) collective-permute-start(bf16[24,4096]{1,0:T(8,128)(2,1)} %reshape.102.refs_4_), channel_id=1, source_target_pairs={{0,10},{2,12},{4,14},{6,0},{8,2},{10,4},{12,6},{14,8},{1,11},{3,13... | collective-permute-start | bytes 589832 | tf_op jit(solution)/shard_map/ppermute | solution.py:123
  96.2 7.0 %collective-permute-start.7 = (bf16[24,4096]{1,0:T(8,128)(2,1)}, bf16[24,4096]{1,0:T(8,128)(2,1)}, u32[]{:S(2)}, u32[]{:S(2)}) collective-permute-start(bf16[24,4096]{1,0:T(8,128)(2,1)} %reshape.102.refs_4_), channel_id=1, source_target_pairs={{0,6},{2,8},{4,10},{6,12},{8,14},{10,0},{12,2},{14,4},{1,7},{3,9},... | collective-permute-start | bytes 589832 | tf_op jit(solution)/shard_map/ppermute | solution.py:123
  103.3 4.6 %collective-permute-start.1 = (bf16[24,4096]{1,0:T(8,128)(2,1)}, bf16[24,4096]{1,0:T(8,128)(2,1)}, u32[]{:S(2)}, u32[]{:S(2)}) collective-permute-start(bf16[24,4096]{1,0:T(8,128)(2,1)} %reshape.102.refs_4_), channel_id=1, source_target_pairs={{0,12},{2,14},{4,0},{6,2},{8,4},{10,6},{12,8},{14,10},{1,13},{3,15... | collective-permute-start | bytes 589832 | tf_op jit(solution)/shard_map/ppermute | solution.py:123
  107.9 2.5 %collective-permute-start.2 = (bf16[24,4096]{1,0:T(8,128)(2,1)}, bf16[24,4096]{1,0:T(8,128)(2,1)}, u32[]{:S(2)}, u32[]{:S(2)}) collective-permute-start(bf16[24,4096]{1,0:T(8,128)(2,1)} %reshape.102.refs_4_), channel_id=1, source_target_pairs={{0,4},{2,6},{4,8},{6,10},{8,12},{10,14},{12,0},{14,2},{1,5},{3,7},... | collective-permute-start | bytes 589832 | tf_op jit(solution)/shard_map/ppermute | solution.py:123
  110.3 10.0 %collective-permute-done.6.refs_1_ = bf16[24,4096]{1,0:T(8,128)(2,1)S(1)} collective-permute-done((bf16[24,4096]{1,0:T(8,128)(2,1)}, bf16[24,4096]{1,0:T(8,128)(2,1)S(1)}, u32[]{:S(2)}, u32[]{:S(2)}) %collective-permute-start.6) | collective-permute-done | bytes 196640 | tf_op jit(solution)/shard_map/ppermute | solution.py:123
  120.3 0.7 copy-done.1
  121.0 1.9 collective-permute-start.3
  122.9 3.9 %collective-permute-start.4 = (bf16[24,4096]{1,0:T(8,128)(2,1)}, bf16[24,4096]{1,0:T(8,128)(2,1)}, u32[]{:S(2)}, u32[]{:S(2)}) collective-permute-start(bf16[24,4096]{1,0:T(8,128)(2,1)} %reshape.102.refs_4_), channel_id=1, source_target_pairs={{0,2},{2,4},{4,6},{6,8},{8,10},{10,12},{12,14},{14,0},{1,3},{3,5},... | collective-permute-start | bytes 589832 | tf_op jit(solution)/shard_map/ppermute | solution.py:123
  126.9 0.7 reshape.100.x_own
  127.6 2.5 %reshape.101.x_other = bf16[384,2048]{1,0:T(8,128)(2,1)S(1)} reshape(bf16[64,96,128]{2,1,0:T(8,128)(2,1)} %collective-permute-done) | data formatting | bytes 3145728 | tf_op jit(solution)/shard_map/reshape | solution.py:210
  130.2 0.9 copy-done.2
  131.1 5.4 %shard_map.103 = (bf16[24,4096]{1,0:T(8,128)(2,1)}, bf16[24,4096]{1,0:T(8,128)(2,1)S(1)}, bf16[24,4096]{1,0:T(8,128)(2,1)S(1)}) custom-call(s32[2]{0:T(128)S(1)} %pad_add_fusion.place, bf16[384,2048]{1,0:T(8,128)(2,1)S(1)} %reshape.100.x_own, bf16[384,2048]{1,0:T(8,128)(2,1)S(1)} %reshape.101.x_other, bf16[24,4096]{1,0:T(8,128)(2,1)S(1)} %collective-permute-done.5.refs_0_, ...), custom_call_target="tpu_custom_call" | custom-call | flops 905969664 | bytes 5242880 | tf_op jit(solution)/shard_map/pallas_call | solution.py:109
  136.5 0.7 copy-done.3
  137.2 0.7 copy-done.5
  137.8 4.1 %collective-permute-start.10 = (bf16[24,4096]{1,0:T(8,128)(2,1)}, bf16[24,4096]{1,0:T(8,128)(2,1)}, u32[]{:S(2)}, u32[]{:S(2)}) collective-permute-start(bf16[24,4096]{1,0:T(8,128)(2,1)} %get-tuple-element.22), channel_id=1, source_target_pairs={{0,4},{1,13},{2,6},{3,15},{4,8},{5,1},{6,10},{7,3},{8,12},{9,5},{1... | collective-permute-start | bytes 589832 | tf_op jit(solution)/shard_map/ppermute | solution.py:131
  142.0 5.8 %shard_map.102 = (bf16[24,4096]{1,0:T(8,128)(2,1)S(1)}, bf16[24,4096]{1,0:T(8,128)(2,1)S(1)}, bf16[24,4096]{1,0:T(8,128)(2,1)S(1)}, bf16[24,4096]{1,0:T(8,128)(2,1)S(1)}, bf16[24,4096]{1,0:T(8,128)(2,1)S(1)}) custom-call(s32[2]{0:T(128)S(1)} %pad_add_fusion.place, bf16[384,2048]{1,0:T(8,128)(2,1)S(1)} %reshape.100.x_own, ...), custom_call_target="tpu_custom_call" | custom-call | flops 1509949440 | bytes 5242880 | tf_op jit(solution)/shard_map/pallas_call | solution.py:109
  147.8 2.4 %collective-permute-start.14 = (bf16[24,4096]{1,0:T(8,128)(2,1)S(1)}, bf16[24,4096]{1,0:T(8,128)(2,1)S(1)}, u32[]{:S(2)}, u32[]{:S(2)}) collective-permute-start(bf16[24,4096]{1,0:T(8,128)(2,1)S(1)} %get-tuple-element.25), channel_id=1, source_target_pairs={{0,14},{2,0},{4,2},{6,4},{8,6},{10,8},{12,10},{14,12},{1,15},{3,1}... | collective-permute-start | bytes 589832 | tf_op jit(solution)/shard_map/ppermute | solution.py:123
  150.2 4.6 %collective-permute-start.13 = (bf16[24,4096]{1,0:T(8,128)(2,1)S(1)}, bf16[24,4096]{1,0:T(8,128)(2,1)S(1)}, u32[]{:S(2)}, u32[]{:S(2)}) collective-permute-start(bf16[24,4096]{1,0:T(8,128)(2,1)S(1)} %get-tuple-element.24), channel_id=1, source_target_pairs={{0,2},{2,4},{4,6},{6,8},{8,10},{10,12},{12,14},{14,0},{1,3},{3,5},... | collective-permute-start | bytes 589832 | tf_op jit(solution)/shard_map/ppermute | solution.py:123
  154.9 3.2 %collective-permute-start.9 = (bf16[24,4096]{1,0:T(8,128)(2,1)S(1)}, bf16[24,4096]{1,0:T(8,128)(2,1)S(1)}, u32[]{:S(2)}, u32[]{:S(2)}) collective-permute-start(bf16[24,4096]{1,0:T(8,128)(2,1)S(1)} %copy-done.6), channel_id=1, source_target_pairs={{0,10},{2,12},{4,14},{6,0},{8,2},{10,4},{12,6},{14,8},{1,11},{3,13... | collective-permute-start | bytes 589832 | tf_op jit(solution)/shard_map/ppermute | solution.py:123
  158.1 4.4 %collective-permute-start.8 = (bf16[24,4096]{1,0:T(8,128)(2,1)S(1)}, bf16[24,4096]{1,0:T(8,128)(2,1)S(1)}, u32[]{:S(2)}, u32[]{:S(2)}) collective-permute-start(bf16[24,4096]{1,0:T(8,128)(2,1)S(1)} %copy-done.4), channel_id=1, source_target_pairs={{0,6},{2,8},{4,10},{6,12},{8,14},{10,0},{12,2},{14,4},{1,7},{3,9},... | collective-permute-start | bytes 589832 | tf_op jit(solution)/shard_map/ppermute | solution.py:123
  162.5 1.0 fusion.1
  163.6 4.0 %collective-permute-start.12 = (bf16[24,4096]{1,0:T(8,128)(2,1)S(1)}, bf16[24,4096]{1,0:T(8,128)(2,1)S(1)}, u32[]{:S(2)}, u32[]{:S(2)}) collective-permute-start(bf16[24,4096]{1,0:T(8,128)(2,1)S(1)} %get-tuple-element.34), channel_id=1, source_target_pairs={{0,12},{2,14},{4,0},{6,2},{8,4},{10,6},{12,8},{14,10},{1,13},{3,15... | collective-permute-start | bytes 589832 | tf_op jit(solution)/shard_map/ppermute | solution.py:123
  167.7 2.9 %collective-permute-start.11 = (bf16[24,4096]{1,0:T(8,128)(2,1)S(1)}, bf16[24,4096]{1,0:T(8,128)(2,1)S(1)}, u32[]{:S(2)}, u32[]{:S(2)}) collective-permute-start(bf16[24,4096]{1,0:T(8,128)(2,1)S(1)} %get-tuple-element.33), channel_id=1, source_target_pairs={{0,4},{2,6},{4,8},{6,10},{8,12},{10,14},{12,0},{14,2},{1,5},{3,7},... | collective-permute-start | bytes 589832 | tf_op jit(solution)/shard_map/ppermute | solution.py:123
  170.5 2.4 %collective-permute-done.9 = bf16[24,4096]{1,0:T(8,128)(2,1)S(1)} collective-permute-done((bf16[24,4096]{1,0:T(8,128)(2,1)S(1)}, bf16[24,4096]{1,0:T(8,128)(2,1)S(1)}, u32[]{:S(2)}, u32[]{:S(2)}) %collective-permute-start.9) | collective-permute-done | bytes 196640 | tf_op jit(solution)/shard_map/ppermute | solution.py:123
  172.9 3.8 %collective-permute-done.8 = bf16[24,4096]{1,0:T(8,128)(2,1)S(1)} collective-permute-done((bf16[24,4096]{1,0:T(8,128)(2,1)S(1)}, bf16[24,4096]{1,0:T(8,128)(2,1)S(1)}, u32[]{:S(2)}, u32[]{:S(2)}) %collective-permute-start.8) | collective-permute-done | bytes 196640 | tf_op jit(solution)/shard_map/ppermute | solution.py:123
  176.7 3.5 %collective-permute-done.12 = bf16[24,4096]{1,0:T(8,128)(2,1)S(1)} collective-permute-done((bf16[24,4096]{1,0:T(8,128)(2,1)S(1)}, bf16[24,4096]{1,0:T(8,128)(2,1)S(1)}, u32[]{:S(2)}, u32[]{:S(2)}) %collective-permute-start.12) | collective-permute-done | bytes 196640 | tf_op jit(solution)/shard_map/ppermute | solution.py:123
  180.2 5.5 %collective-permute-done.11 = bf16[24,4096]{1,0:T(8,128)(2,1)S(1)} collective-permute-done((bf16[24,4096]{1,0:T(8,128)(2,1)S(1)}, bf16[24,4096]{1,0:T(8,128)(2,1)S(1)}, u32[]{:S(2)}, u32[]{:S(2)}) %collective-permute-start.11) | collective-permute-done | bytes 196640 | tf_op jit(solution)/shard_map/ppermute | solution.py:123
  185.7 0.9 fusion.21
  186.7 0.3 reshape.103
  186.9 21.4 %all_to_all.16 = bf16[64,12,128]{2,1,0:T(8,128)(2,1)S(1)} all-to-all(bf16[64,12,128]{2,1,0:T(8,128)(2,1)S(1)} %reshape.103), channel_id=1, replica_groups=mesh['expert'=64,'z'=8,'c'=2] {'expert'}, dimensions={0} | all-to-all | bytes 393216 | tf_op jit(solution)/shard_map/all_to_all | solution.py:227
  208.4 1.1 multiply_subtract_fusion
  (35 shorter events, 0.7 us)
Async XLA Ops:
  0.6 24.8 %copy-start = (bf16[16,8,384]{2,1,0:T(8,128)(2,1)S(1)}, bf16[16,8,384]{2,1,0:T(8,128)(2,1)}, u32[]{:S(2)}) copy-start(bf16[16,8,384]{2,1,0:T(8,128)(2,1)} %param.8) | copy-start | bytes 294916
  2.7 30.4 %all-to-all-start = ((bf16[64,12,128]{2,1,0:T(8,128)(2,1)}), bf16[64,12,128]{2,1,0:T(8,128)(2,1)S(1)}, u32[]{:S(2)}, u32[]{:S(2)}) async-start(bf16[64,12,128]{2,1,0:T(8,128)(2,1)} %reshape.99), calls=%async_computation | async-start | bytes 524288 | tf_op jit(solution)/shard_map/all_to_all | solution.py:164
  75.8 47.1 %collective-permute-start = (bf16[64,96,128]{2,1,0:T(8,128)(2,1)S(1)}, bf16[64,96,128]{2,1,0:T(8,128)(2,1)}, u32[]{:S(2)}, u32[]{:S(2)}) collective-permute-start(bf16[64,96,128]{2,1,0:T(8,128)(2,1)S(1)} %all_to_all.15), channel_id=1, source_target_pairs={{0,1},{1,0},{2,3},{3,2},{4,5},{5,4},{6,7},{7,6},{8,9},{9,8},{10,11... | collective-permute-start | bytes 4718600 | tf_op jit(solution)/shard_map/ppermute | solution.py:202
  78.6 29.2 %collective-permute-start.5 = (bf16[24,4096]{1,0:T(8,128)(2,1)}, bf16[24,4096]{1,0:T(8,128)(2,1)S(1)}, u32[]{:S(2)}, u32[]{:S(2)}) collective-permute-start(bf16[24,4096]{1,0:T(8,128)(2,1)} %reshape.102.refs_4_), channel_id=1, source_target_pairs={{0,8},{2,10},{4,12},{6,14},{8,0},{10,2},{12,4},{14,6},{1,9},{3,11}... | collective-permute-start | bytes 589832 | tf_op jit(solution)/shard_map/ppermute | solution.py:123
  93.4 26.9 %collective-permute-start.6 = (bf16[24,4096]{1,0:T(8,128)(2,1)}, bf16[24,4096]{1,0:T(8,128)(2,1)S(1)}, u32[]{:S(2)}, u32[]{:S(2)}) collective-permute-start(bf16[24,4096]{1,0:T(8,128)(2,1)} %reshape.102.refs_4_), channel_id=1, source_target_pairs={{0,10},{2,12},{4,14},{6,0},{8,2},{10,4},{12,6},{14,8},{1,11},{3,13... | collective-permute-start | bytes 589832 | tf_op jit(solution)/shard_map/ppermute | solution.py:123
  96.2 34.0 %collective-permute-start.7 = (bf16[24,4096]{1,0:T(8,128)(2,1)}, bf16[24,4096]{1,0:T(8,128)(2,1)}, u32[]{:S(2)}, u32[]{:S(2)}) collective-permute-start(bf16[24,4096]{1,0:T(8,128)(2,1)} %reshape.102.refs_4_), channel_id=1, source_target_pairs={{0,6},{2,8},{4,10},{6,12},{8,14},{10,0},{12,2},{14,4},{1,7},{3,9},... | collective-permute-start | bytes 589832 | tf_op jit(solution)/shard_map/ppermute | solution.py:123
  103.3 38.7 %collective-permute-start.1 = (bf16[24,4096]{1,0:T(8,128)(2,1)}, bf16[24,4096]{1,0:T(8,128)(2,1)}, u32[]{:S(2)}, u32[]{:S(2)}) collective-permute-start(bf16[24,4096]{1,0:T(8,128)(2,1)} %reshape.102.refs_4_), channel_id=1, source_target_pairs={{0,12},{2,14},{4,0},{6,2},{8,4},{10,6},{12,8},{14,10},{1,13},{3,15... | collective-permute-start | bytes 589832 | tf_op jit(solution)/shard_map/ppermute | solution.py:123
  107.9 34.1 %collective-permute-start.2 = (bf16[24,4096]{1,0:T(8,128)(2,1)}, bf16[24,4096]{1,0:T(8,128)(2,1)}, u32[]{:S(2)}, u32[]{:S(2)}) collective-permute-start(bf16[24,4096]{1,0:T(8,128)(2,1)} %reshape.102.refs_4_), channel_id=1, source_target_pairs={{0,4},{2,6},{4,8},{6,10},{8,12},{10,14},{12,0},{14,2},{1,5},{3,7},... | collective-permute-start | bytes 589832 | tf_op jit(solution)/shard_map/ppermute | solution.py:123
  120.3 0.7 copy-start.1
  121.0 21.0 %collective-permute-start.3 = (bf16[24,4096]{1,0:T(8,128)(2,1)}, bf16[24,4096]{1,0:T(8,128)(2,1)}, u32[]{:S(2)}, u32[]{:S(2)}) collective-permute-start(bf16[24,4096]{1,0:T(8,128)(2,1)} %reshape.102.refs_4_), channel_id=1, source_target_pairs={{0,14},{2,0},{4,2},{6,4},{8,6},{10,8},{12,10},{14,12},{1,15},{3,1}... | collective-permute-start | bytes 589832 | tf_op jit(solution)/shard_map/ppermute | solution.py:123
  122.9 19.1 %collective-permute-start.4 = (bf16[24,4096]{1,0:T(8,128)(2,1)}, bf16[24,4096]{1,0:T(8,128)(2,1)}, u32[]{:S(2)}, u32[]{:S(2)}) collective-permute-start(bf16[24,4096]{1,0:T(8,128)(2,1)} %reshape.102.refs_4_), channel_id=1, source_target_pairs={{0,2},{2,4},{4,6},{6,8},{8,10},{10,12},{12,14},{14,0},{1,3},{3,5},... | collective-permute-start | bytes 589832 | tf_op jit(solution)/shard_map/ppermute | solution.py:123
  130.2 0.9 copy-start.2
  136.5 0.7 copy-start.3
  137.2 0.7 copy-start.5
  137.8 24.7 %collective-permute-start.10 = (bf16[24,4096]{1,0:T(8,128)(2,1)}, bf16[24,4096]{1,0:T(8,128)(2,1)}, u32[]{:S(2)}, u32[]{:S(2)}) collective-permute-start(bf16[24,4096]{1,0:T(8,128)(2,1)} %get-tuple-element.22), channel_id=1, source_target_pairs={{0,4},{1,13},{2,6},{3,15},{4,8},{5,1},{6,10},{7,3},{8,12},{9,5},{1... | collective-permute-start | bytes 589832 | tf_op jit(solution)/shard_map/ppermute | solution.py:131
  141.9 12.9 %copy-start.6 = (bf16[24,4096]{1,0:T(8,128)(2,1)S(1)}, bf16[24,4096]{1,0:T(8,128)(2,1)}, u32[]{:S(2)}) copy-start(bf16[24,4096]{1,0:T(8,128)(2,1)} %copy-done.5) | copy-start | bytes 589828
  141.9 16.1 %copy-start.4 = (bf16[24,4096]{1,0:T(8,128)(2,1)S(1)}, bf16[24,4096]{1,0:T(8,128)(2,1)}, u32[]{:S(2)}) copy-start(bf16[24,4096]{1,0:T(8,128)(2,1)} %copy-done.3) | copy-start | bytes 589828
  147.8 19.9 %collective-permute-start.14 = (bf16[24,4096]{1,0:T(8,128)(2,1)S(1)}, bf16[24,4096]{1,0:T(8,128)(2,1)S(1)}, u32[]{:S(2)}, u32[]{:S(2)}) collective-permute-start(bf16[24,4096]{1,0:T(8,128)(2,1)S(1)} %get-tuple-element.25), channel_id=1, source_target_pairs={{0,14},{2,0},{4,2},{6,4},{8,6},{10,8},{12,10},{14,12},{1,15},{3,1}... | collective-permute-start | bytes 589832 | tf_op jit(solution)/shard_map/ppermute | solution.py:123
  150.2 20.3 %collective-permute-start.13 = (bf16[24,4096]{1,0:T(8,128)(2,1)S(1)}, bf16[24,4096]{1,0:T(8,128)(2,1)S(1)}, u32[]{:S(2)}, u32[]{:S(2)}) collective-permute-start(bf16[24,4096]{1,0:T(8,128)(2,1)S(1)} %get-tuple-element.24), channel_id=1, source_target_pairs={{0,2},{2,4},{4,6},{6,8},{8,10},{10,12},{12,14},{14,0},{1,3},{3,5},... | collective-permute-start | bytes 589832 | tf_op jit(solution)/shard_map/ppermute | solution.py:123
  154.9 18.1 %collective-permute-start.9 = (bf16[24,4096]{1,0:T(8,128)(2,1)S(1)}, bf16[24,4096]{1,0:T(8,128)(2,1)S(1)}, u32[]{:S(2)}, u32[]{:S(2)}) collective-permute-start(bf16[24,4096]{1,0:T(8,128)(2,1)S(1)} %copy-done.6), channel_id=1, source_target_pairs={{0,10},{2,12},{4,14},{6,0},{8,2},{10,4},{12,6},{14,8},{1,11},{3,13... | collective-permute-start | bytes 589832 | tf_op jit(solution)/shard_map/ppermute | solution.py:123
  158.1 18.7 %collective-permute-start.8 = (bf16[24,4096]{1,0:T(8,128)(2,1)S(1)}, bf16[24,4096]{1,0:T(8,128)(2,1)S(1)}, u32[]{:S(2)}, u32[]{:S(2)}) collective-permute-start(bf16[24,4096]{1,0:T(8,128)(2,1)S(1)} %copy-done.4), channel_id=1, source_target_pairs={{0,6},{2,8},{4,10},{6,12},{8,14},{10,0},{12,2},{14,4},{1,7},{3,9},... | collective-permute-start | bytes 589832 | tf_op jit(solution)/shard_map/ppermute | solution.py:123
  163.6 44.8 %copy-start.7 = (f32[32,1536]{1,0:T(8,128)S(1)}, f32[32,1536]{1,0:T(8,128)}, u32[]{:S(2)}) copy-start(f32[32,1536]{1,0:T(8,128)} %param.11) | copy-start | bytes 589828
  163.6 44.8 %copy-start.8 = (s32[64]{0:T(128)S(1)}, s32[64]{0:T(128)}, u32[]{:S(2)}) copy-start(s32[64]{0:T(128)} %param.10) | copy-start | bytes 772
  163.6 44.7 %copy-start.9 = (f32[32,1536]{1,0:T(8,128)S(1)}, f32[32,1536]{1,0:T(8,128)}, u32[]{:S(2)}) copy-start(f32[32,1536]{1,0:T(8,128)} %param.12) | copy-start | bytes 589828
  163.6 44.7 %copy-start.10 = (f32[32,1536]{1,0:T(8,128)S(1)}, f32[32,1536]{1,0:T(8,128)}, u32[]{:S(2)}) copy-start(f32[32,1536]{1,0:T(8,128)} %param.13) | copy-start | bytes 589828
  163.6 16.6 %collective-permute-start.12 = (bf16[24,4096]{1,0:T(8,128)(2,1)S(1)}, bf16[24,4096]{1,0:T(8,128)(2,1)S(1)}, u32[]{:S(2)}, u32[]{:S(2)}) collective-permute-start(bf16[24,4096]{1,0:T(8,128)(2,1)S(1)} %get-tuple-element.34), channel_id=1, source_target_pairs={{0,12},{2,14},{4,0},{6,2},{8,4},{10,6},{12,8},{14,10},{1,13},{3,15... | collective-permute-start | bytes 589832 | tf_op jit(solution)/shard_map/ppermute | solution.py:123
  167.7 18.1 %collective-permute-start.11 = (bf16[24,4096]{1,0:T(8,128)(2,1)S(1)}, bf16[24,4096]{1,0:T(8,128)(2,1)S(1)}, u32[]{:S(2)}, u32[]{:S(2)}) collective-permute-start(bf16[24,4096]{1,0:T(8,128)(2,1)S(1)} %get-tuple-element.33), channel_id=1, source_target_pairs={{0,4},{2,6},{4,8},{6,10},{8,12},{10,14},{12,0},{14,2},{1,5},{3,7},... | collective-permute-start | bytes 589832 | tf_op jit(solution)/shard_map/ppermute | solution.py:123
where the time goes:
time: 210 us; the launch traced here: 209 us
  starting transfers between devices  82.3 us (39%)
  blocking collectives  64.1 us (31%)
  waiting for transfers between devices  31.4 us (15%)
  Pallas kernels  11.1 us (5%)
  local copies, waits for them, and re-layouts  10 us (5%)
  other arithmetic  5.35 us (3%)
  matrix products  4.15 us (2%)
    ppermute x13, starting transfers between devices, shift(): lax.ppermute(value, 'z', [(i, (i - by) % planes) for i in range(planes)])  59.1 us
    all_to_all x1, blocking collectives, local(): lax.all_to_all(send, 'expert', split_axis=0, concat_axis=0, tiled=True)  42.7 us
    ppermute x13, waiting for transfers between devices, shift(): lax.ppermute(value, 'z', [(i, (i - by) % planes) for i in range(planes)])  25.2 us
    all_to_all x1, blocking collectives, local(): lax.all_to_all(outgoing, 'expert', split_axis=0, concat_axis=0, tiled=True)  21.4 us
    all_to_all x1, starting transfers between devices, local(): lax.all_to_all(send_weight, 'expert', split_axis=0, concat_axis=0, tiled=...  17.2 us
    pallas_call x2, Pallas kernels, swiglu_grads(): pl.pallas_call(functools.partial(grads_kernel, planes, piece_rows, first_...  11.1 us
    all_to_all x1, waiting for transfers between devices, local(): lax.all_to_all(send_weight, 'expert', split_axis=0, concat_axis=0, tiled=...  6.2 us
  transfers between devices with their start and end apart: 16, of which 6 were waited for; matrix products, arithmetic and copies ran while one was open for 6% of the time, Pallas kernels for 5%

commit v1 on v0

--- a/solution.py
+++ b/solution.py
@@ -39,23 +39,26 @@
     return jnp.where(block % 2 == 1, (planes - 1 - block) // 2, -((planes - block) // 2))
 
 
-def store_grads(outs, parts, rows_refs, piece_rows, width):
+def store_grads(outs, parts, rows_refs, units, width):
     tile = 512
-    units = len(outs) * piece_rows
     for start in range(0, width, tile):
         cols = slice(start, start + tile)
         total = jnp.dot(parts[0], rows_refs[0][:, cols], preferred_element_type=jnp.float32)
         total += jnp.dot(parts[1], rows_refs[1][:, cols], preferred_element_type=jnp.float32)
         total = total.reshape(2, units, tile)
-        for at, out in enumerate(outs):
-            rows = slice(at * piece_rows, (at + 1) * piece_rows)
-            out[:, start : start + tile] = total[0, rows].astype(jnp.bfloat16)
-            out[:, width + start : width + start + tile] = total[1, rows].astype(jnp.bfloat16)
-
-
-def grads_kernel(planes, piece_rows, first_block, count, place, x_own, x_other, *refs):
+        for out, lines in outs:
+            to = 0
+            for first, end in lines:
+                rows = slice(to, to + end - first)
+                out[rows, start : start + tile] = total[0, first:end].astype(jnp.bfloat16)
+                more = slice(width + start, width + start + tile)
+                out[rows, more] = total[1, first:end].astype(jnp.bfloat16)
+                to += end - first
+
+
+def grads_kernel(planes, piece_rows, first_block, count, lines_of, place, x_own, x_other, *refs):
     f32, bf16 = jnp.float32, jnp.bfloat16
-    pieces, outs, weights = refs[:count], refs[count : 2 * count], refs[2 * count]
+    pieces, outs, weights = refs[:count], refs[count:-1], refs[-1]
     units, width = weights.shape[0] // 2, weights.shape[1]
     for at, piece in enumerate(pieces):
         lines = slice(at * piece_rows, (at + 1) * piece_rows)
@@ -96,21 +99,24 @@
         d_gate = dh * up * (sig * (1.0 + gate * (1.0 - sig)))
         d_up = dh * (gate * sig)
         parts.append(jnp.concatenate([d_gate, d_up], axis=0).astype(bf16))
-    store_grads(outs, parts, (x_own, x_other), piece_rows, width)
-
-
-def swiglu_grads(planes, piece_rows, first_block, place, x_own, x_other, pieces):
+    store_grads(list(zip(outs, lines_of)), parts, (x_own, x_other), units, width)
+
+
+def swiglu_grads(planes, piece_rows, first_block, place, x_own, x_other, pieces, lines_of):
     bf16 = jnp.bfloat16
     vmem, smem = pl.BlockSpec(memory_space=pltpu.VMEM), pl.BlockSpec(memory_space=pltpu.SMEM)
     rows, width = x_own.shape
     count = len(pieces)
     units = count * piece_rows
-    block = jax.ShapeDtypeStruct((piece_rows, 2 * width), bf16)
+    blocks = [
+        jax.ShapeDtypeStruct((sum(end - first for first, end in lines), 2 * width), bf16)
+        for lines in lines_of
+    ]
     return pl.pallas_call(
-        functools.partial(grads_kernel, planes, piece_rows, first_block, count),
-        out_shape=[block] * count,
+        functools.partial(grads_kernel, planes, piece_rows, first_block, count, lines_of),
+        out_shape=blocks,
         in_specs=[smem] + [vmem] * (2 + count),
-        out_specs=[vmem] * count,
+        out_specs=[vmem] * len(blocks),
         scratch_shapes=[pltpu.VMEM((2 * units, width), bf16)],
         compiler_params=pltpu.CompilerParams(vmem_limit_bytes=GRANT),
         cost_estimate=pl.CostEstimate(
@@ -121,14 +127,6 @@
 
 def shift(value, planes, by):
     return lax.ppermute(value, "z", [(i, (i - by) % planes) for i in range(planes)])
-
-
-def shift_by_core(value, planes, by):
-    pairs = []
-    for i in range(planes):
-        pairs.append((i * CORES, (i - by) % planes * CORES))
-        pairs.append((i * CORES + 1, (i + by) % planes * CORES + 1))
-    return lax.ppermute(value, ("z", "c"), pairs)
 
 
 def gather_planes(piece, planes):
@@ -208,15 +206,26 @@
     place = jnp.stack([lax.axis_index("z"), core])
     x_own = recv.reshape(slots * group, width)
     x_other = other.reshape(slots * group, width)
-    far = swiglu_grads(planes, piece_rows, 0, place, x_own, x_other, pieces[:FAR])
-    relayed = shift_by_core(far[0], planes, -2)
-    parts = [shift(far[1], planes, -3), shift(far[2], planes, 3)]
-    near = swiglu_grads(planes, piece_rows, FAR, place, x_own, x_other, pieces[FAR:])
+    part = piece_rows // 3 * 2
+    far_lines = (
+        ((piece_rows, 2 * piece_rows), (0, part)),
+        ((2 * piece_rows, 3 * piece_rows), (part, piece_rows)),
+    )
+    near_lines = tuple(((k * piece_rows, (k + 1) * piece_rows),) for k in range(planes - FAR))
+    above, below = swiglu_grads(
+        planes, piece_rows, 0, place, x_own, x_other, pieces[:FAR], far_lines
+    )
+    above, below = shift(above, planes, -2), shift(below, planes, 2)
+    near = swiglu_grads(planes, piece_rows, FAR, place, x_own, x_other, pieces[FAR:], near_lines)
     up2, down2, up1, down1, own = near
-    more = relayed.astype(f32)
-    up2 = (up2.astype(f32) + jnp.where(core == 0, more, 0.0)).astype(bf16)
-    down2 = (down2.astype(f32) + jnp.where(core == 0, 0.0, more)).astype(bf16)
-    parts += [shift(up2, planes, -2), shift(down2, planes, 2)]
+    above, below = above.astype(f32), below.astype(f32)
+    over = jnp.pad(above[piece_rows:], ((0, piece_rows - part), (0, 0)))
+    under = jnp.pad(below[piece_rows:], ((part, 0), (0, 0)))
+    up2 = (up2.astype(f32) + over).astype(bf16)
+    down2 = (down2.astype(f32) + under).astype(bf16)
+    up1 = (up1.astype(f32) + above[:piece_rows]).astype(bf16)
+    down1 = (down1.astype(f32) + below[:piece_rows]).astype(bf16)
+    parts = [shift(up2, planes, -2), shift(down2, planes, 2)]
     parts += [shift(up1, planes, -1), shift(down1, planes, 1)]
     summed = own.astype(f32)
     for part in parts:

time: 210 us -> 194 us (0.924)
  waiting for transfers between devices: 31.4 us -> 25.3 us
  starting transfers between devices: 82.3 us -> 77.7 us
  local copies, waits for them, and re-layouts: 10 us -> 7.11 us
    ppermute x13, waiting for transfers between devices: 25.2 us -> 19.1 us  [shift(): lax.ppermute(value, 'z', [(i, (i - by) % planes) for i in range(planes)])]
    ppermute x1 -> x0, starting transfers between devices: 4.08 us -> none  [shift_by_core(): return lax.ppermute(value, ('z', 'c'), pairs)]
    unnamed x23 -> x11, local copies, waits for them, and re-layouts: 3.76 us -> 0.8 us
  transfers between devices with their start and end apart: 16 -> 15, of which waited for: 6 -> 7; matrix products, arithmetic and copies ran while one was open for 6% -> 6% of each run, Pallas kernels for 5% -> 5%
where the time goes in v1:
time: 194 us; the launch traced here: 193 us
  starting transfers between devices  77.7 us (40%)
  blocking collectives  62.9 us (32%)
  waiting for transfers between devices  25.3 us (13%)
  Pallas kernels  10.3 us (5%)
  local copies, waits for them, and re-layouts  7.11 us (4%)
  other arithmetic  4.46 us (2%)
  matrix products  4.15 us (2%)
    ppermute x13, starting transfers between devices, shift(): lax.ppermute(value, 'z', [(i, (i - by) % planes) for i in range(planes)])  58.6 us
    all_to_all x1, blocking collectives, local(): lax.all_to_all(send, 'expert', split_axis=0, concat_axis=0, tiled=True)  42.7 us
    all_to_all x1, blocking collectives, local(): lax.all_to_all(outgoing, 'expert', split_axis=0, concat_axis=0, tiled=True)  20.2 us
    ppermute x13, waiting for transfers between devices, shift(): lax.ppermute(value, 'z', [(i, (i - by) % planes) for i in range(planes)])  19.1 us
    all_to_all x1, starting transfers between devices, local(): lax.all_to_all(send_weight, 'expert', split_axis=0, concat_axis=0, tiled=...  17.2 us
    pallas_call x2, Pallas kernels, swiglu_grads(): pl.pallas_call(functools.partial(grads_kernel, planes, piece_rows, first_...  10.3 us
    all_to_all x1, waiting for transfers between devices, local(): lax.all_to_all(send_weight, 'expert', split_axis=0, concat_axis=0, tiled=...  6.2 us
  transfers between devices with their start and end apart: 15, of which 7 were waited for; matrix products, arithmetic and copies ran while one was open for 6% of the time, Pallas kernels for 5%

profile of v1, /device:TPU:2, one launch (start us, length us, event | category | flops | bytes accessed | tf_op | source)
XLA Modules:
  0.0 193.0 jit_solution(5771981740345521058)
XLA Ops:
  0.6 1.2 convolution_convert_fusion.1
  1.9 0.9 reshape.99
  2.7 17.2 %all-to-all-start = ((bf16[64,12,128]{2,1,0:T(8,128)(2,1)}), bf16[64,12,128]{2,1,0:T(8,128)(2,1)S(1)}, u32[]{:S(2)}, u32[]{:S(2)}) async-start(bf16[64,12,128]{2,1,0:T(8,128)(2,1)} %reshape.99), calls=%async_computation | async-start | bytes 524288 | tf_op jit(solution)/shard_map/all_to_all | solution.py:162
  20.0 0.8 convert_reduce_fusion.2
  20.7 0.9 convert_reduce_fusion.1
  21.6 0.8 copy.13
  22.4 0.1 eq.105
  22.5 0.2 convert_reduce_fusion
  22.7 0.1 and_select_fusion.1
  22.8 0.8 select_reduce_fusion.1
  23.6 0.1 select_reduce_fusion
  23.7 1.6 convolution_convert_fusion
  25.4 0.6 reshape.96
  26.0 0.2 convolution_convert_fusion.2
  26.3 0.2 reshape.98
  26.4 0.1 pad.12.clone
  26.5 0.4 maximum_maximum_fusion
  26.9 6.2 %all-to-all-done = bf16[64,12,128]{2,1,0:T(8,128)(2,1)S(1)} async-done(((bf16[64,12,128]{2,1,0:T(8,128)(2,1)}), bf16[64,12,128]{2,1,0:T(8,128)(2,1)S(1)}, u32[]{:S(2)}, u32[]{:S(2)}) %all-to-all-start) | async-done | bytes 196640 | tf_op jit(solution)/shard_map/all_to_all | solution.py:162
  33.1 42.7 %all_to_all.15 = bf16[64,96,128]{2,1,0:T(8,128)(2,1)S(1)} all-to-all(bf16[64,96,128]{2,1,0:T(8,128)(2,1)S(1)} %maximum_maximum_fusion), channel_id=1, replica_groups=mesh['expert'=64,'z'=8,'c'=2] {'expert'}, dimensions={0} | all-to-all | bytes 3145728 | tf_op jit(solution)/shard_map/all_to_all | solution.py:199
  75.8 1.9 collective-permute-start
  77.7 0.9 reshape.102.refs_4_
  78.6 14.8 %collective-permute-start.5 = (bf16[24,4096]{1,0:T(8,128)(2,1)}, bf16[24,4096]{1,0:T(8,128)(2,1)S(1)}, u32[]{:S(2)}, u32[]{:S(2)}) collective-permute-start(bf16[24,4096]{1,0:T(8,128)(2,1)} %reshape.102.refs_4_), channel_id=1, source_target_pairs={{0,8},{2,10},{4,12},{6,14},{8,0},{10,2},{12,4},{14,6},{1,9},{3,11}... | collective-permute-start | bytes 589832 | tf_op jit(solution)/shard_map/ppermute | solution.py:129
  93.4 2.8 %collective-permute-start.6 = (bf16[24,4096]{1,0:T(8,128)(2,1)}, bf16[24,4096]{1,0:T(8,128)(2,1)}, u32[]{:S(2)}, u32[]{:S(2)}) collective-permute-start(bf16[24,4096]{1,0:T(8,128)(2,1)} %reshape.102.refs_4_), channel_id=1, source_target_pairs={{0,10},{2,12},{4,14},{6,0},{8,2},{10,4},{12,6},{14,8},{1,11},{3,13... | collective-permute-start | bytes 589832 | tf_op jit(solution)/shard_map/ppermute | solution.py:129
  96.2 7.0 %collective-permute-start.7 = (bf16[24,4096]{1,0:T(8,128)(2,1)}, bf16[24,4096]{1,0:T(8,128)(2,1)}, u32[]{:S(2)}, u32[]{:S(2)}) collective-permute-start(bf16[24,4096]{1,0:T(8,128)(2,1)} %reshape.102.refs_4_), channel_id=1, source_target_pairs={{0,6},{2,8},{4,10},{6,12},{8,14},{10,0},{12,2},{14,4},{1,7},{3,9},... | collective-permute-start | bytes 589832 | tf_op jit(solution)/shard_map/ppermute | solution.py:129
  103.3 4.6 %collective-permute-start.1 = (bf16[24,4096]{1,0:T(8,128)(2,1)}, bf16[24,4096]{1,0:T(8,128)(2,1)}, u32[]{:S(2)}, u32[]{:S(2)}) collective-permute-start(bf16[24,4096]{1,0:T(8,128)(2,1)} %reshape.102.refs_4_), channel_id=1, source_target_pairs={{0,12},{2,14},{4,0},{6,2},{8,4},{10,6},{12,8},{14,10},{1,13},{3,15... | collective-permute-start | bytes 589832 | tf_op jit(solution)/shard_map/ppermute | solution.py:129
  107.9 0.7 reshape.100.x_own
  108.7 2.5 %collective-permute-start.2 = (bf16[24,4096]{1,0:T(8,128)(2,1)}, bf16[24,4096]{1,0:T(8,128)(2,1)}, u32[]{:S(2)}, u32[]{:S(2)}) collective-permute-start(bf16[24,4096]{1,0:T(8,128)(2,1)} %reshape.102.refs_4_), channel_id=1, source_target_pairs={{0,4},{2,6},{4,8},{6,10},{8,12},{10,14},{12,0},{14,2},{1,5},{3,7},... | collective-permute-start | bytes 589832 | tf_op jit(solution)/shard_map/ppermute | solution.py:129
  111.1 2.5 %reshape.101.x_other = bf16[384,2048]{1,0:T(8,128)(2,1)S(1)} reshape(bf16[64,96,128]{2,1,0:T(8,128)(2,1)} %collective-permute-done) | data formatting | bytes 3145728 | tf_op jit(solution)/shard_map/reshape | solution.py:208
  113.7 4.6 %collective-permute-start.3 = (bf16[24,4096]{1,0:T(8,128)(2,1)}, bf16[24,4096]{1,0:T(8,128)(2,1)S(1)}, u32[]{:S(2)}, u32[]{:S(2)}) collective-permute-start(bf16[24,4096]{1,0:T(8,128)(2,1)} %reshape.102.refs_4_), channel_id=1, source_target_pairs={{0,14},{2,0},{4,2},{6,4},{8,6},{10,8},{12,10},{14,12},{1,15},{3,1}... | collective-permute-start | bytes 589832 | tf_op jit(solution)/shard_map/ppermute | solution.py:129
  118.3 2.1 %collective-permute-done.6.refs_1_ = bf16[24,4096]{1,0:T(8,128)(2,1)} collective-permute-done((bf16[24,4096]{1,0:T(8,128)(2,1)}, bf16[24,4096]{1,0:T(8,128)(2,1)}, u32[]{:S(2)}, u32[]{:S(2)}) %collective-permute-start.6) | collective-permute-done | bytes 196640 | tf_op jit(solution)/shard_map/ppermute | solution.py:129
  120.4 1.9 collective-permute-start.4
  122.3 4.8 %shard_map.103 = (bf16[40,4096]{1,0:T(8,128)(2,1)S(1)}, bf16[32,4096]{1,0:T(8,128)(2,1)S(1)}) custom-call(s32[2]{0:T(128)S(1)} %pad_add_fusion.place, bf16[384,2048]{1,0:T(8,128)(2,1)S(1)} %reshape.100.x_own, bf16[384,2048]{1,0:T(8,128)(2,1)S(1)} %reshape.101.x_other, bf16[24,4096]{1,0:T(8,128)(2,1)S(1)} %collective-permute-done.5.refs_0_, ...), custom_call_target="tpu_custom_call" | custom-call | flops 905969664 | bytes 5242880 | tf_op jit(solution)/shard_map/pallas_call | solution.py:115
  127.1 7.8 %collective-permute-start.10 = (bf16[32,4096]{1,0:T(8,128)(2,1)S(1)}, bf16[32,4096]{1,0:T(8,128)(2,1)S(1)}, u32[]{:S(2)}, u32[]{:S(2)}) collective-permute-start(bf16[32,4096]{1,0:T(8,128)(2,1)S(1)} %get-tuple-element.21), channel_id=1, source_target_pairs={{0,12},{2,14},{4,0},{6,2},{8,4},{10,6},{12,8},{14,10},{1,13},{3,15... | collective-permute-start | bytes 786440 | tf_op jit(solution)/shard_map/ppermute | solution.py:129
  134.9 1.9 collective-permute-start.8
  136.9 5.5 %shard_map.102 = (bf16[24,4096]{1,0:T(8,128)(2,1)S(1)}, bf16[24,4096]{1,0:T(8,128)(2,1)S(1)}, bf16[24,4096]{1,0:T(8,128)(2,1)S(1)}, bf16[24,4096]{1,0:T(8,128)(2,1)S(1)}, bf16[24,4096]{1,0:T(8,128)(2,1)S(1)}) custom-call(s32[2]{0:T(128)S(1)} %pad_add_fusion.place, bf16[384,2048]{1,0:T(8,128)(2,1)S(1)} %reshape.100.x_own, ...), custom_call_target="tpu_custom_call" | custom-call | flops 1509949440 | bytes 5242880 | tf_op jit(solution)/shard_map/pallas_call | solution.py:115
  142.4 2.3 %collective-permute-done.10 = bf16[32,4096]{1,0:T(8,128)(2,1)S(1)} collective-permute-done((bf16[32,4096]{1,0:T(8,128)(2,1)S(1)}, bf16[32,4096]{1,0:T(8,128)(2,1)S(1)}, u32[]{:S(2)}, u32[]{:S(2)}) %collective-permute-start.10) | collective-permute-done | bytes 262176 | tf_op jit(solution)/shard_map/ppermute | solution.py:129
  144.8 4.4 %collective-permute-start.11 = (bf16[24,4096]{1,0:T(8,128)(2,1)S(1)}, bf16[24,4096]{1,0:T(8,128)(2,1)S(1)}, u32[]{:S(2)}, u32[]{:S(2)}) collective-permute-start(bf16[24,4096]{1,0:T(8,128)(2,1)S(1)} %add_convert_fusion), channel_id=1, source_target_pairs={{0,12},{2,14},{4,0},{6,2},{8,4},{10,6},{12,8},{14,10},{1,13},{3,15... | collective-permute-start | bytes 589832 | tf_op jit(solution)/shard_map/ppermute | solution.py:129
  149.3 1.9 collective-permute-start.13
  151.2 2.0 %collective-permute-done.8 = bf16[40,4096]{1,0:T(8,128)(2,1)S(1)} collective-permute-done((bf16[40,4096]{1,0:T(8,128)(2,1)S(1)}, bf16[40,4096]{1,0:T(8,128)(2,1)S(1)}, u32[]{:S(2)}, u32[]{:S(2)}) %collective-permute-start.8) | collective-permute-done | bytes 327712 | tf_op jit(solution)/shard_map/ppermute | solution.py:129
  153.3 1.9 collective-permute-start.9
  155.3 2.5 %collective-permute-start.12 = (bf16[24,4096]{1,0:T(8,128)(2,1)S(1)}, bf16[24,4096]{1,0:T(8,128)(2,1)S(1)}, u32[]{:S(2)}, u32[]{:S(2)}) collective-permute-start(bf16[24,4096]{1,0:T(8,128)(2,1)S(1)} %fusion.1), channel_id=1, source_target_pairs={{0,2},{2,4},{4,6},{6,8},{8,10},{10,12},{12,14},{14,0},{1,3},{3,5},... | collective-permute-start | bytes 589832 | tf_op jit(solution)/shard_map/ppermute | solution.py:129
  157.8 2.0 %collective-permute-done.13 = bf16[24,4096]{1,0:T(8,128)(2,1)S(1)} collective-permute-done((bf16[24,4096]{1,0:T(8,128)(2,1)S(1)}, bf16[24,4096]{1,0:T(8,128)(2,1)S(1)}, u32[]{:S(2)}, u32[]{:S(2)}) %collective-permute-start.13) | collective-permute-done | bytes 196640 | tf_op jit(solution)/shard_map/ppermute | solution.py:129
  159.8 8.2 %collective-permute-done.9 = bf16[24,4096]{1,0:T(8,128)(2,1)S(1)} collective-permute-done((bf16[24,4096]{1,0:T(8,128)(2,1)S(1)}, bf16[24,4096]{1,0:T(8,128)(2,1)S(1)}, u32[]{:S(2)}, u32[]{:S(2)}) %collective-permute-start.9) | collective-permute-done | bytes 196640 | tf_op jit(solution)/shard_map/ppermute | solution.py:129
  168.0 2.5 %collective-permute-done.12 = bf16[24,4096]{1,0:T(8,128)(2,1)S(1)} collective-permute-done((bf16[24,4096]{1,0:T(8,128)(2,1)S(1)}, bf16[24,4096]{1,0:T(8,128)(2,1)S(1)}, u32[]{:S(2)}, u32[]{:S(2)}) %collective-permute-start.12) | collective-permute-done | bytes 196640 | tf_op jit(solution)/shard_map/ppermute | solution.py:129
  170.5 0.9 fusion.18
  171.4 0.3 reshape.103
  171.7 20.2 %all_to_all.16 = bf16[64,12,128]{2,1,0:T(8,128)(2,1)S(1)} all-to-all(bf16[64,12,128]{2,1,0:T(8,128)(2,1)S(1)} %reshape.103), channel_id=1, replica_groups=mesh['expert'=64,'z'=8,'c'=2] {'expert'}, dimensions={0} | all-to-all | bytes 393216 | tf_op jit(solution)/shard_map/all_to_all | solution.py:236
  191.9 1.1 multiply_subtract_fusion
  (28 shorter events, 0.4 us)
Async XLA Ops:
  0.6 25.4 %copy-start = (bf16[16,8,384]{2,1,0:T(8,128)(2,1)S(1)}, bf16[16,8,384]{2,1,0:T(8,128)(2,1)}, u32[]{:S(2)}) copy-start(bf16[16,8,384]{2,1,0:T(8,128)(2,1)} %param.8) | copy-start | bytes 294916
  2.7 30.4 %all-to-all-start = ((bf16[64,12,128]{2,1,0:T(8,128)(2,1)}), bf16[64,12,128]{2,1,0:T(8,128)(2,1)S(1)}, u32[]{:S(2)}, u32[]{:S(2)}) async-start(bf16[64,12,128]{2,1,0:T(8,128)(2,1)} %reshape.99), calls=%async_computation | async-start | bytes 524288 | tf_op jit(solution)/shard_map/all_to_all | solution.py:162
  75.8 32.9 %collective-permute-start = (bf16[64,96,128]{2,1,0:T(8,128)(2,1)S(1)}, bf16[64,96,128]{2,1,0:T(8,128)(2,1)}, u32[]{:S(2)}, u32[]{:S(2)}) collective-permute-start(bf16[64,96,128]{2,1,0:T(8,128)(2,1)S(1)} %all_to_all.15), channel_id=1, source_target_pairs={{0,1},{1,0},{2,3},{3,2},{4,5},{5,4},{6,7},{7,6},{8,9},{9,8},{10,11... | collective-permute-start | bytes 4718600 | tf_op jit(solution)/shard_map/ppermute | solution.py:200
  78.6 35.1 %collective-permute-start.5 = (bf16[24,4096]{1,0:T(8,128)(2,1)}, bf16[24,4096]{1,0:T(8,128)(2,1)S(1)}, u32[]{:S(2)}, u32[]{:S(2)}) collective-permute-start(bf16[24,4096]{1,0:T(8,128)(2,1)} %reshape.102.refs_4_), channel_id=1, source_target_pairs={{0,8},{2,10},{4,12},{6,14},{8,0},{10,2},{12,4},{14,6},{1,9},{3,11}... | collective-permute-start | bytes 589832 | tf_op jit(solution)/shard_map/ppermute | solution.py:129
  93.4 27.0 %collective-permute-start.6 = (bf16[24,4096]{1,0:T(8,128)(2,1)}, bf16[24,4096]{1,0:T(8,128)(2,1)}, u32[]{:S(2)}, u32[]{:S(2)}) collective-permute-start(bf16[24,4096]{1,0:T(8,128)(2,1)} %reshape.102.refs_4_), channel_id=1, source_target_pairs={{0,10},{2,12},{4,14},{6,0},{8,2},{10,4},{12,6},{14,8},{1,11},{3,13... | collective-permute-start | bytes 589832 | tf_op jit(solution)/shard_map/ppermute | solution.py:129
  96.2 26.1 %collective-permute-start.7 = (bf16[24,4096]{1,0:T(8,128)(2,1)}, bf16[24,4096]{1,0:T(8,128)(2,1)}, u32[]{:S(2)}, u32[]{:S(2)}) collective-permute-start(bf16[24,4096]{1,0:T(8,128)(2,1)} %reshape.102.refs_4_), channel_id=1, source_target_pairs={{0,6},{2,8},{4,10},{6,12},{8,14},{10,0},{12,2},{14,4},{1,7},{3,9},... | collective-permute-start | bytes 589832 | tf_op jit(solution)/shard_map/ppermute | solution.py:129
  103.3 31.6 %collective-permute-start.1 = (bf16[24,4096]{1,0:T(8,128)(2,1)}, bf16[24,4096]{1,0:T(8,128)(2,1)}, u32[]{:S(2)}, u32[]{:S(2)}) collective-permute-start(bf16[24,4096]{1,0:T(8,128)(2,1)} %reshape.102.refs_4_), channel_id=1, source_target_pairs={{0,12},{2,14},{4,0},{6,2},{8,4},{10,6},{12,8},{14,10},{1,13},{3,15... | collective-permute-start | bytes 589832 | tf_op jit(solution)/shard_map/ppermute | solution.py:129
  108.7 28.2 %collective-permute-start.2 = (bf16[24,4096]{1,0:T(8,128)(2,1)}, bf16[24,4096]{1,0:T(8,128)(2,1)}, u32[]{:S(2)}, u32[]{:S(2)}) collective-permute-start(bf16[24,4096]{1,0:T(8,128)(2,1)} %reshape.102.refs_4_), channel_id=1, source_target_pairs={{0,4},{2,6},{4,8},{6,10},{8,12},{10,14},{12,0},{14,2},{1,5},{3,7},... | collective-permute-start | bytes 589832 | tf_op jit(solution)/shard_map/ppermute | solution.py:129
  113.7 23.2 %collective-permute-start.3 = (bf16[24,4096]{1,0:T(8,128)(2,1)}, bf16[24,4096]{1,0:T(8,128)(2,1)S(1)}, u32[]{:S(2)}, u32[]{:S(2)}) collective-permute-start(bf16[24,4096]{1,0:T(8,128)(2,1)} %reshape.102.refs_4_), channel_id=1, source_target_pairs={{0,14},{2,0},{4,2},{6,4},{8,6},{10,8},{12,10},{14,12},{1,15},{3,1}... | collective-permute-start | bytes 589832 | tf_op jit(solution)/shard_map/ppermute | solution.py:129
  120.4 16.5 %collective-permute-start.4 = (bf16[24,4096]{1,0:T(8,128)(2,1)}, bf16[24,4096]{1,0:T(8,128)(2,1)S(1)}, u32[]{:S(2)}, u32[]{:S(2)}) collective-permute-start(bf16[24,4096]{1,0:T(8,128)(2,1)} %reshape.102.refs_4_), channel_id=1, source_target_pairs={{0,2},{2,4},{4,6},{6,8},{8,10},{10,12},{12,14},{14,0},{1,3},{3,5},... | collective-permute-start | bytes 589832 | tf_op jit(solution)/shard_map/ppermute | solution.py:129
  127.1 17.6 %collective-permute-start.10 = (bf16[32,4096]{1,0:T(8,128)(2,1)S(1)}, bf16[32,4096]{1,0:T(8,128)(2,1)S(1)}, u32[]{:S(2)}, u32[]{:S(2)}) collective-permute-start(bf16[32,4096]{1,0:T(8,128)(2,1)S(1)} %get-tuple-element.21), channel_id=1, source_target_pairs={{0,12},{2,14},{4,0},{6,2},{8,4},{10,6},{12,8},{14,10},{1,13},{3,15... | collective-permute-start | bytes 786440 | tf_op jit(solution)/shard_map/ppermute | solution.py:129
  134.9 18.3 %collective-permute-start.8 = (bf16[40,4096]{1,0:T(8,128)(2,1)S(1)}, bf16[40,4096]{1,0:T(8,128)(2,1)S(1)}, u32[]{:S(2)}, u32[]{:S(2)}) collective-permute-start(bf16[40,4096]{1,0:T(8,128)(2,1)S(1)} %get-tuple-element.19), channel_id=1, source_target_pairs={{0,4},{2,6},{4,8},{6,10},{8,12},{10,14},{12,0},{14,2},{1,5},{3,7},... | collective-permute-start | bytes 983048 | tf_op jit(solution)/shard_map/ppermute | solution.py:129
  144.8 13.1 %collective-permute-start.11 = (bf16[24,4096]{1,0:T(8,128)(2,1)S(1)}, bf16[24,4096]{1,0:T(8,128)(2,1)S(1)}, u32[]{:S(2)}, u32[]{:S(2)}) collective-permute-start(bf16[24,4096]{1,0:T(8,128)(2,1)S(1)} %add_convert_fusion), channel_id=1, source_target_pairs={{0,12},{2,14},{4,0},{6,2},{8,4},{10,6},{12,8},{14,10},{1,13},{3,15... | collective-permute-start | bytes 589832 | tf_op jit(solution)/shard_map/ppermute | solution.py:129
  149.3 10.5 %collective-permute-start.13 = (bf16[24,4096]{1,0:T(8,128)(2,1)S(1)}, bf16[24,4096]{1,0:T(8,128)(2,1)S(1)}, u32[]{:S(2)}, u32[]{:S(2)}) collective-permute-start(bf16[24,4096]{1,0:T(8,128)(2,1)S(1)} %fusion), channel_id=1, source_target_pairs={{0,14},{2,0},{4,2},{6,4},{8,6},{10,8},{12,10},{14,12},{1,15},{3,1}... | collective-permute-start | bytes 589832 | tf_op jit(solution)/shard_map/ppermute | solution.py:129
  153.3 14.7 %collective-permute-start.9 = (bf16[24,4096]{1,0:T(8,128)(2,1)S(1)}, bf16[24,4096]{1,0:T(8,128)(2,1)S(1)}, u32[]{:S(2)}, u32[]{:S(2)}) collective-permute-start(bf16[24,4096]{1,0:T(8,128)(2,1)S(1)} %add_convert_fusion.1), channel_id=1, source_target_pairs={{0,4},{2,6},{4,8},{6,10},{8,12},{10,14},{12,0},{14,2},{1,5},{3,7},... | collective-permute-start | bytes 589832 | tf_op jit(solution)/shard_map/ppermute | solution.py:129
  155.2 36.7 %copy-start.1 = (f32[32,1536]{1,0:T(8,128)S(1)}, f32[32,1536]{1,0:T(8,128)}, u32[]{:S(2)}) copy-start(f32[32,1536]{1,0:T(8,128)} %param.11) | copy-start | bytes 589828
  155.3 36.6 %copy-start.2 = (s32[64]{0:T(128)S(1)}, s32[64]{0:T(128)}, u32[]{:S(2)}) copy-start(s32[64]{0:T(128)} %param.10) | copy-start | bytes 772
  155.3 36.6 %copy-start.3 = (f32[32,1536]{1,0:T(8,128)S(1)}, f32[32,1536]{1,0:T(8,128)}, u32[]{:S(2)}) copy-start(f32[32,1536]{1,0:T(8,128)} %param.12) | copy-start | bytes 589828
  155.3 36.6 %copy-start.4 = (f32[32,1536]{1,0:T(8,128)S(1)}, f32[32,1536]{1,0:T(8,128)}, u32[]{:S(2)}) copy-start(f32[32,1536]{1,0:T(8,128)} %param.13) | copy-start | bytes 589828
  155.3 15.2 %collective-permute-start.12 = (bf16[24,4096]{1,0:T(8,128)(2,1)S(1)}, bf16[24,4096]{1,0:T(8,128)(2,1)S(1)}, u32[]{:S(2)}, u32[]{:S(2)}) collective-permute-start(bf16[24,4096]{1,0:T(8,128)(2,1)S(1)} %fusion.1), channel_id=1, source_target_pairs={{0,2},{2,4},{4,6},{6,8},{8,10},{10,12},{12,14},{14,0},{1,3},{3,5},... | collective-permute-start | bytes 589832 | tf_op jit(solution)/shard_map/ppermute | solution.py:129
